TPU v7x, 512 devices: a whole 4x8x8 slice. The times are simulated.
512 devices in a mesh: seq: 32 (over z_lo, y, core), head: 16 (over x, z_hi).
Axes of the slice: x: 4, y: 8, z: 8 (z_hi: 4, z_lo: 2; z = z_hi * 2 + z_lo), core: 2. Of those that a mesh axis runs over, the one named last changes fastest.
Arguments:
- q_nope: bfloat16 [3072, 16384], P('seq', 'head'), may hold values from -6 to 6
- q_rope: bfloat16 [3072, 8192], P('seq', 'head'), may hold values from -48 to 48
- w_uk: bfloat16 [128, 128, 512], P('head'), may hold values from -0.5 to 0.5
- w_uv: bfloat16 [128, 512, 128], P('head'), may hold values from -0.25 to 0.25
- w_value: float32 [16384], P('head'), may hold values from -0.1875 to 0.1875
- kv_cache: bfloat16 [4096, 576], P('seq'), may hold values from -8 to 8
- cutoffs: int32 [3072], P('seq'), may hold values from 1 to 4096, as said below
Outputs:
- attn: bfloat16 [3072, 16384], P('seq', 'head')
- value: float32 [3072], P('seq')
Inputs may be any that keep to these rules, and one draw needn't show every extreme that they name: `cutoffs`: every row sees at least the first event; some row sees the whole history and some row only the first event.
All inputs are finite; a program needn't handle non-finite values.
Results may differ from a plain program's by a relative error of at most 0.014.
Values may be sent and summed in bfloat16 or wider, within the bound.
A program may use at most 64 MiB of HBM per device.

v0:
```python
import jax
import jax.numpy as jnp
from jax import lax
from jax.sharding import PartitionSpec as P

softmax_scale = (128.0 + 64.0) ** (-0.5)


def on_device(q_nope, q_rope, w_uk, w_uv, w_value, kv_cache, cutoffs):
    rows = q_nope.shape[0]
    heads = w_uk.shape[0]
    latent = w_uk.shape[2]
    nope_rows = q_nope.reshape(rows, heads, w_uk.shape[1])
    q_lat = jnp.einsum("rhn,hnc->rhc", nope_rows, w_uk, preferred_element_type=jnp.float32).astype(
        jnp.bfloat16
    )
    q_all = jnp.concatenate([q_lat, q_rope.reshape(rows, heads, -1)], axis=2)
    piece = lax.all_gather(kv_cache, "seq", axis=0, tiled=True)
    running = jnp.full((rows, heads), -1e30, jnp.float32)
    count = piece.shape[0]
    score = (
        jnp.einsum("rhc,ec->rhe", q_all, piece, preferred_element_type=jnp.float32) * softmax_scale
    )
    index = jnp.arange(count, dtype=jnp.int32)
    keep = index[None, None, :] < cutoffs[:, None, None]
    score = jnp.where(keep, score, -jnp.inf)
    newest = jnp.maximum(running, jnp.max(score, axis=2))
    weight = jnp.exp(score - newest[:, :, None])
    total = jnp.sum(weight, axis=2)
    update = jnp.einsum(
        "rhe,ec->rhc",
        weight.astype(jnp.bfloat16),
        piece[:, :latent],
        preferred_element_type=jnp.float32,
    )
    accum = update
    running, total, accum = (newest, total, accum)
    o_lat = (accum / total[:, :, None]).astype(jnp.bfloat16)
    attn = jnp.einsum("rhc,hcv->rhv", o_lat, w_uv, preferred_element_type=jnp.float32).astype(
        jnp.bfloat16
    )
    attn = attn.reshape(rows, -1)
    partial_score = jnp.sum(attn.astype(jnp.float32) * w_value[None, :], axis=1)
    value = lax.psum(partial_score, "head")
    return (attn, value)


def solution(mesh):
    placed = (
        P("seq", "head"),
        P("seq", "head"),
        P("head", None, None),
        P("head", None, None),
        P("head"),
        P("seq", None),
        P("seq"),
    )
    return jax.shard_map(
        on_device,
        mesh=mesh,
        in_specs=placed,
        out_specs=(P("seq", "head"), P("seq")),
        check_vma=False,
    )
```

profile of v0, /device:TPU:16, one launch (start us, length us, event | category | flops | bytes accessed | tf_op | source)
XLA Modules:
  0.0 163.2 jit_solution(10106467120380042580)
XLA Ops:
  7.2 0.0 copy-start
  7.2 0.0 all-gather.2.cloned.1.call-start
  7.2 0.7 all-gather.2.cloned.1.call-update
  7.9 1.0 copy.13
  8.9 0.2 copy.14
  9.1 0.0 copy-done
  9.1 1.3 fusion.11
  10.4 0.1 pad_maximum_fusion
  10.5 1.0 iota_compare_fusion
  11.4 79.9 %all-gather.2.cloned.1.call-done = bf16[4096,576]{0,1:T(8,128)(2,1)} async-done(((bf16[128,576]{0,1:T(8,128)(2,1)}), bf16[4096,576]{0,1:T(8,128)(2,1)}) %all-gather.2.cloned.1.call-update) | async-done | bytes 4718608 | tf_op jit(solution)/shard_map/all_gather | solution.py:18
  91.3 8.0 %fusion = (f32[96,8]{1,0:T(8,128)S(1)}, f32[96,8,4096]{2,1,0:T(8,128)S(1)}) fusion(pred[96,4096]{1,0:T(8,128)(4,1)S(1)} %iota_compare_fusion, bf16[4096,576]{0,1:T(8,128)(2,1)} %all-gather.2.cloned.1.call-done, bf16[96,8,576]{2,0,1:T(8,128)(2,1)S(1)} %pad_maximum_fusion), kind=kOutput, calls=%fused_computation.2 | convolution fusion | flops 3633315072 | bytes 18582528 | tf_op jit(solution)/shard_map/rhc,ec->rhe/dot_general | solution.py:22
  99.3 3.9 %fusion.1 = f32[96,8]{1,0:T(8,128)S(1)} fusion(f32[96,8,4096]{2,1,0:T(8,128)S(1)} %get-tuple-element.3, f32[96,8]{1,0:T(8,128)S(1)} %broadcast_maximum_fusion, pred[96,4096]{1,0:T(8,128)(4,1)S(1)} %iota_compare_fusion), kind=kLoop, calls=%fused_computation.3 | loop fusion | flops 12582144 | bytes 12982272 | tf_op jit(solution)/shard_map/reduce_sum | solution.py:29
  103.2 0.0 copy-start.1
  103.2 0.0 copy-start.2
  103.2 6.1 %divide_convert_fusion = bf16[96,8,512]{2,1,0:T(8,128)(2,1)S(1)} fusion(bf16[4096,576]{0,1:T(8,128)(2,1)} %all-gather.2.cloned.1.call-done, f32[96,8,4096]{2,1,0:T(8,128)S(1)} %get-tuple-element.3, f32[96,8]{1,0:T(8,128)S(1)} %broadcast_maximum_fusion, pred[96,4096]{1,0:T(8,128)(4,1)S(1)} %iota_compare_fusion, f32[96,8]{1,0:T(8,128)S(1)} %fusion.1), kind=kOutput, calls=%fused_computation.13 | convolution fusion | flops 3234594816 | bytes 17963008 | tf_op jit(solution)/shard_map/rhe,ec->rhc/dot_general | solution.py:30
  109.3 0.0 copy-done.1
  109.3 0.0 copy-done.2
  109.3 0.7 multiply_reduce_fusion
  110.0 45.7 %psum.7 = f32[96]{0:T(128)} all-reduce(f32[96]{0:T(128)S(1)} %get-tuple-element.4), channel_id=1, replica_groups=mesh['seq'=32,'head'=16] {'head'}, use_global_device_ids=true, to_apply=%region_3.4 | all-reduce | flops 96 | bytes 768 | tf_op jit(solution)/shard_map/psum | solution.py:44
  155.7 0.7 copy_bitcast_fusion
  (1 shorter events, 0.0 us)
Async XLA Ops:
  7.2 1.9 %copy-start = (bf16[8,128,512]{2,1,0:T(8,128)(2,1)S(1)}, bf16[8,128,512]{2,1,0:T(8,128)(2,1)}, u32[]{:S(2)}) copy-start(bf16[8,128,512]{2,1,0:T(8,128)(2,1)} %param.9) | copy-start | bytes 3145732
  7.2 84.1 %all-gather.2.cloned.1.call-start = ((), (), s32[]{:S(2)}) async-start(), calls=%async_computation | async-start | bytes 4866048 | tf_op jit(solution)/shard_map/all_gather | solution.py:18
  103.2 6.1 %copy-start.1 = (bf16[8,512,128]{2,1,0:T(8,128)(2,1)S(1)}, bf16[8,512,128]{2,1,0:T(8,128)(2,1)}, u32[]{:S(2)}) copy-start(bf16[8,512,128]{2,1,0:T(8,128)(2,1)} %param.10) | copy-start | bytes 3145732
  103.2 6.1 %copy-start.2 = (f32[1024]{0:T(1024)S(1)}, f32[1024]{0:T(1024)}, u32[]{:S(2)}) copy-start(f32[1024]{0:T(1024)} %param.11) | copy-start | bytes 12292
Sparse Core Ops, SparseCore 0:
  10.1 81.1 all-gather.1
where the time goes:
time: 163 us
  waiting for transfers between devices  80.5 us (49%)
  blocking collectives  45.7 us (28%)
  matrix products  16 us (10%)
  between operations  14.1 us (9%)
  other arithmetic  4.93 us (3%)
  local copies, waits for them, and re-layouts  1.87 us (1%)
    all_gather x1, waiting for transfers between devices, on_device(): piece = lax.all_gather(kv_cache, 'seq', axis=0, tiled=True)  79.9 us
    psum x1, blocking collectives, on_device(): value = lax.psum(partial_score, 'head')  45.7 us
    dot_general x1, matrix products, on_device(): jnp.einsum('rhc,ec->rhe', q_all, piece, preferred_element_type=jnp.float32)  7.95 us
    dot_general x1, matrix products, on_device(): jnp.einsum('rhe,ec->rhc', weight.astype(jnp.bfloat16), piece[:, :latent],...  6.09 us
    reduce_sum x1, other arithmetic, on_device(): total = jnp.sum(weight, axis=2)  3.89 us
  transfers between devices with their start and end apart: 1, of which 1 were waited for; matrix products, arithmetic and copies ran while one was open for 2% of the time, Pallas kernels for 0%

commit v1 on v0

--- a/solution.py
+++ b/solution.py
@@ -7,6 +7,13 @@
 
 
 def on_device(q_nope, q_rope, w_uk, w_uv, w_value, kv_cache, cutoffs):
+
+    def watch_terms_all(point):
+        return jnp.concatenate(
+            lax.all_to_all(jnp.stack([point for _ in range(lax.axis_size("seq"))], 0), "seq", 0, 0),
+            0,
+        )
+
     rows = q_nope.shape[0]
     heads = w_uk.shape[0]
     latent = w_uk.shape[2]
@@ -15,7 +22,7 @@
         jnp.bfloat16
     )
     q_all = jnp.concatenate([q_lat, q_rope.reshape(rows, heads, -1)], axis=2)
-    piece = lax.all_gather(kv_cache, "seq", axis=0, tiled=True)
+    piece = watch_terms_all(kv_cache)
     running = jnp.full((rows, heads), -1e30, jnp.float32)
     count = piece.shape[0]
     score = (

time: 163 us -> 212 us (1.30)
  the two profiles are of different devices: /device:TPU:16 before, /device:TPU:24 now
where the time goes in v1:
time: 212 us
  waiting for transfers between devices  106 us (50%)
  blocking collectives  49.1 us (23%)
  local copies, waits for them, and re-layouts  26.1 us (12%)
  matrix products  15.1 us (7%)
  starting transfers between devices  10.2 us (5%)
  other arithmetic  4.42 us (2%)
    all_to_all x1, waiting for transfers between devices, watch_terms_all(): lax.all_to_all(jnp.stack([point for _ in range(lax.axis_size('seq'))], 0)...  106 us
    psum x1, blocking collectives, on_device(): value = lax.psum(partial_score, 'head')  49.1 us
    reshape x2, local copies, waits for them, and re-layouts, watch_terms_all(): jnp.concatenate(lax.all_to_all(jnp.stack([point for _ in range(lax.axis_s...  13.4 us
    all_to_all x1, starting transfers between devices, watch_terms_all(): lax.all_to_all(jnp.stack([point for _ in range(lax.axis_size('seq'))], 0)...  10.2 us
    dot_general x1, matrix products, on_device(): jnp.einsum('rhc,ec->rhe', q_all, piece, preferred_element_type=jnp.float32)  7.94 us
    all_to_all x1, local copies, waits for them, and re-layouts, watch_terms_all(): lax.all_to_all(jnp.stack([point for _ in range(lax.axis_size('seq'))], 0)...  7.54 us
    dot_general x1, matrix products, on_device(): jnp.einsum('rhe,ec->rhc', weight.astype(jnp.bfloat16), piece[:, :latent],...  6.09 us
  transfers between devices with their start and end apart: 1, of which 1 were waited for; matrix products, arithmetic and copies ran while one was open for 0% of the time, Pallas kernels for 0%

profile of v1, /device:TPU:24, one launch (start us, length us, event | category | flops | bytes accessed | tf_op | source)
XLA Modules:
  0.0 212.0 jit_solution(3584351704391941209)
XLA Ops:
  0.6 0.0 copy-start
  0.6 4.2 %stack.2 = bf16[32,128,576]{1,2,0:T(8,128)(2,1)} broadcast(bf16[128,576]{0,1:T(8,128)(2,1)} %param.12), dimensions={1,2} | broadcast | bytes 4866048 | tf_op jit(solution)/shard_map/stack | solution.py:13
  4.9 0.0 copy-start.2
  4.9 0.0 copy-start.1
  4.9 0.0 copy-start.3
  4.9 10.2 %all-to-all-start = ((bf16[32,128,576]{1,2,0:T(8,128)(2,1)}), bf16[32,128,576]{1,2,0:T(8,128)(2,1)}, u32[]{:S(2)}, u32[]{:S(2)}) async-start(bf16[32,128,576]{1,2,0:T(8,128)(2,1)} %stack.2), calls=%async_computation | async-start | bytes 9437184 | tf_op jit(solution)/shard_map/all_to_all | solution.py:13
  15.1 0.0 copy-done.2
  15.1 0.1 copy.13
  15.2 0.2 copy.14
  15.4 0.0 copy-done
  15.4 0.0 copy-done.1
  15.4 0.4 fusion.9
  15.8 0.1 pad_maximum_fusion
  15.9 0.0 copy-done.3
  15.9 0.3 iota_compare_fusion
  16.2 106.3 %all-to-all-done = bf16[32,128,576]{1,2,0:T(8,128)(2,1)} async-done(((bf16[32,128,576]{1,2,0:T(8,128)(2,1)}), bf16[32,128,576]{1,2,0:T(8,128)(2,1)}, u32[]{:S(2)}, u32[]{:S(2)}) %all-to-all-start) | async-done | bytes 4718624 | tf_op jit(solution)/shard_map/all_to_all | solution.py:13
  122.4 7.5 %copy.15 = bf16[32,128,576]{1,0,2:T(8,128)(2,1)} copy(bf16[32,128,576]{1,2,0:T(8,128)(2,1)} %all-to-all-done) | data formatting | bytes 9437184 | tf_op jit(solution)/shard_map/all_to_all | solution.py:13
  130.0 8.2 %reshape.53 = bf16[4096,576,1]{0,1,2:T(8,128)(2,1)} reshape(bf16[32,128,576]{1,0,2:T(8,128)(2,1)} %copy.15) | data formatting | bytes 9437184 | tf_op jit(solution)/shard_map/reshape | solution.py:12
  138.1 7.9 %fusion = (f32[96,8]{1,0:T(8,128)S(1)}, f32[96,8,4096]{2,1,0:T(8,128)S(1)}) fusion(pred[96,4096]{1,0:T(8,128)(4,1)S(1)} %iota_compare_fusion, bf16[4096,576,1]{0,1,2:T(8,128)(2,1)} %reshape.53, bf16[96,8,576]{2,0,1:T(8,128)(2,1)S(1)} %pad_maximum_fusion), kind=kOutput, calls=%fused_computation.2 | convolution fusion | flops 3633315072 | bytes 18582528 | tf_op jit(solution)/shard_map/rhc,ec->rhe/dot_general | solution.py:29
  146.1 4.0 %fusion.1 = f32[96,8]{1,0:T(8,128)S(1)} fusion(f32[96,8,4096]{2,1,0:T(8,128)S(1)} %get-tuple-element.3, f32[96,8]{1,0:T(8,128)S(1)} %broadcast_maximum_fusion, pred[96,4096]{1,0:T(8,128)(4,1)S(1)} %iota_compare_fusion), kind=kLoop, calls=%fused_computation.3 | loop fusion | flops 12582144 | bytes 12982272 | tf_op jit(solution)/shard_map/reduce_sum | solution.py:36
  150.1 5.2 %copy_bitcast_fusion = bf16[4096,576]{0,1:T(8,128)(2,1)} fusion(bf16[32,128,576]{1,2,0:T(8,128)(2,1)} %all-to-all-done), kind=kLoop, calls=%fused_computation.10 | loop fusion | bytes 9437184 | tf_op jit(solution)/shard_map/reshape | solution.py:12
  155.3 0.0 copy-start.4
  155.4 0.0 copy-start.5
  155.4 6.1 %divide_convert_fusion = bf16[96,8,512]{2,1,0:T(8,128)(2,1)S(1)} fusion(bf16[4096,576]{0,1:T(8,128)(2,1)} %copy_bitcast_fusion, f32[96,8,4096]{2,1,0:T(8,128)S(1)} %get-tuple-element.3, f32[96,8]{1,0:T(8,128)S(1)} %broadcast_maximum_fusion, pred[96,4096]{1,0:T(8,128)(4,1)S(1)} %iota_compare_fusion, f32[96,8]{1,0:T(8,128)S(1)} %fusion.1), kind=kOutput, calls=%fused_computation.12 | convolution fusion | flops 3234594816 | bytes 17963008 | tf_op jit(solution)/shard_map/rhe,ec->rhc/dot_general | solution.py:37
  161.5 0.0 copy-done.4
  161.5 0.0 copy-done.5
  161.5 0.7 multiply_reduce_fusion
  162.2 49.1 %psum.7 = f32[96]{0:T(128)} all-reduce(f32[96]{0:T(128)S(1)} %get-tuple-element.4), channel_id=1, replica_groups=mesh['seq'=32,'head'=16] {'head'}, use_global_device_ids=true, to_apply=%region_3.4 | all-reduce | flops 96 | bytes 768 | tf_op jit(solution)/shard_map/psum | solution.py:51
  211.3 0.7 copy_bitcast_fusion.1
  (1 shorter events, 0.0 us)
Async XLA Ops:
  0.6 14.8 %copy-start = (bf16[8,128,512]{2,1,0:T(8,128)(2,1)S(1)}, bf16[8,128,512]{2,1,0:T(8,128)(2,1)}, u32[]{:S(2)}) copy-start(bf16[8,128,512]{2,1,0:T(8,128)(2,1)} %param.9) | copy-start | bytes 3145732
  4.9 10.2 %copy-start.2 = (bf16[96,512]{1,0:T(8,128)(2,1)S(1)}, bf16[96,512]{1,0:T(8,128)(2,1)}, u32[]{:S(2)}) copy-start(bf16[96,512]{1,0:T(8,128)(2,1)} %param.8) | copy-start | bytes 294916
  4.9 10.5 %copy-start.1 = (bf16[96,1024]{1,0:T(8,128)(2,1)S(1)}, bf16[96,1024]{1,0:T(8,128)(2,1)}, u32[]{:S(2)}) copy-start(bf16[96,1024]{1,0:T(8,128)(2,1)} %param.7) | copy-start | bytes 589828
  4.9 11.0 %copy-start.3 = (s32[96]{0:T(128)S(1)}, s32[96]{0:T(128)}, u32[]{:S(2)}) copy-start(s32[96]{0:T(128)} %param.13) | copy-start | bytes 1156
  4.9 117.6 %all-to-all-start = ((bf16[32,128,576]{1,2,0:T(8,128)(2,1)}), bf16[32,128,576]{1,2,0:T(8,128)(2,1)}, u32[]{:S(2)}, u32[]{:S(2)}) async-start(bf16[32,128,576]{1,2,0:T(8,128)(2,1)} %stack.2), calls=%async_computation | async-start | bytes 9437184 | tf_op jit(solution)/shard_map/all_to_all | solution.py:13
  155.3 6.1 %copy-start.4 = (bf16[8,512,128]{2,1,0:T(8,128)(2,1)S(1)}, bf16[8,512,128]{2,1,0:T(8,128)(2,1)}, u32[]{:S(2)}) copy-start(bf16[8,512,128]{2,1,0:T(8,128)(2,1)} %param.10) | copy-start | bytes 3145732
  155.4 6.1 %copy-start.5 = (f32[1024]{0:T(1024)S(1)}, f32[1024]{0:T(1024)}, u32[]{:S(2)}) copy-start(f32[1024]{0:T(1024)} %param.11) | copy-start | bytes 12292
